TPU v7x, 32 devices: a whole 2x2x4 slice. The times are simulated.
32 devices in a mesh: fsdp: 8 (over y, x, core), cp: 4 (over z).
Axes of the slice: x: 2, y: 2, z: 4, core: 2. Of those that a mesh axis runs over, the one named last changes fastest.
Arguments:
- features: bfloat16 [8, 512, 2560], P('fsdp', 'cp'), may hold values from -6 to 6
- query_rows: bfloat16 [8, 512, 1280], P('fsdp', 'cp'), may hold values from -40 to 40, as said below
- key_rows: bfloat16 [8, 512, 1280], P('fsdp', 'cp'), may hold values from -4 to 4
- value_rows: bfloat16 [8, 512, 1280], P('fsdp', 'cp'), may hold values from -6 to 6
- attn_output: bfloat16 [8, 512, 1280], P('fsdp', 'cp'), may hold values from -6 to 6
- grad_output: bfloat16 [8, 512, 1280], P('fsdp', 'cp'), may hold values from -6 to 6
- log_sums: float32 [8, 512, 10], P('fsdp', 'cp'), as said below
Outputs:
- d_query: bfloat16 [8, 512, 1280], P('fsdp', 'cp')
- d_key: bfloat16 [8, 512, 1280], P('fsdp', 'cp')
- d_value: bfloat16 [8, 512, 1280], P('fsdp', 'cp')
- d_value_weight: float32 [2560, 1280], P('fsdp', 'cp')
Inputs may be any that keep to these rules, and one draw needn't show every extreme that they name: `query_rows`: queries of a clip, with key_rows and log_sums drawn together with them. log_sums[c, t, h] is the logarithm of the sum over all 512 keys u of clip c of exp(128**-0.5 * q[t] . k[u]) for head h, computed from the bfloat16 queries and keys in float32.
All inputs are finite; a program needn't handle non-finite values.
Results may differ from a plain program's by a relative error of at most 0.02.
Values may be sent and summed in bfloat16 or wider, within the bound.
No kernel may reach another device: no remote copies, remote signals or barrier semaphores. Data moves between devices by JAX's collectives and lax.ppermute only.
A program may use at most 128 MiB of HBM per device.

v0:
```python
import jax
import jax.numpy as jnp
from jax import lax
from jax.sharding import PartitionSpec as P


def passed_along(value, axis, steps):
    count = lax.axis_size(axis)
    pairs = [(source, (source + steps) % count) for source in range(count)]
    return lax.ppermute(value, axis, pairs)


def on_device(features, query_rows, key_rows, value_rows, attn_output, grad_output, log_sums):
    rows_here = query_rows.shape[1]
    proj_width = query_rows.shape[2]
    head_count = log_sums.shape[2]
    head_size = proj_width // head_count
    softmax_scale = head_size ** (-0.5)

    def as_heads(block):
        return block[0].reshape(block.shape[1], head_count, head_size)

    product = grad_output.astype(jnp.float32) * attn_output.astype(jnp.float32)
    row_delta = jnp.sum(product.reshape(1, rows_here, head_count, head_size), axis=3)
    own_key = as_heads(key_rows)
    own_value = as_heads(value_rows)
    all_norms, all_deltas = (
        lax.all_gather(log_sums, "cp", axis=1, tiled=True),
        lax.all_gather(row_delta, "cp", axis=1, tiled=True),
    )

    def pair_scores(query_heads, grad_heads, offset, rows_in):
        norm_block = lax.dynamic_slice_in_dim(all_norms, offset, rows_in, 1)[0].T
        delta_block = lax.dynamic_slice_in_dim(all_deltas, offset, rows_in, 1)[0].T
        scores = (
            jnp.einsum("qhd,khd->hqk", query_heads, own_key, preferred_element_type=jnp.float32)
            * softmax_scale
        )
        attn_prob = jnp.exp(scores - norm_block[:, :, None])
        grad_prob = jnp.einsum(
            "qhd,khd->hqk", grad_heads, own_value, preferred_element_type=jnp.float32
        )
        grad_score = (attn_prob * (grad_prob - delta_block[:, :, None])).astype(jnp.bfloat16)
        return (grad_score, attn_prob.astype(jnp.bfloat16))

    zero_rows = jnp.zeros((rows_here, head_count, head_size), jnp.float32)
    position = lax.axis_index("cp")
    cycle_count = lax.axis_size("cp")

    def cycle_step(step, state):
        query_block, grad_block, query_run, key_run, value_run = state
        source = (position - step) % cycle_count
        offset = source * rows_here
        query_heads = as_heads(query_block)
        grad_heads = as_heads(grad_block)
        grad_score, prob_half = pair_scores(query_heads, grad_heads, offset, rows_here)
        query_run = query_run + jnp.einsum(
            "hqk,khd->qhd", grad_score, own_key, preferred_element_type=jnp.float32
        )
        key_run = key_run + jnp.einsum(
            "hqk,qhd->khd", grad_score, query_heads, preferred_element_type=jnp.float32
        )
        value_run = value_run + jnp.einsum(
            "hqk,qhd->khd", prob_half, grad_heads, preferred_element_type=jnp.float32
        )
        query_block, grad_block = passed_along((query_block, grad_block), "cp", 1)
        query_run = passed_along(query_run.astype(jnp.bfloat16), "cp", 1).astype(query_run.dtype)
        return (query_block, grad_block, query_run, key_run, value_run)

    start_state = (query_rows, grad_output, zero_rows, zero_rows, zero_rows)
    final_state = lax.fori_loop(0, cycle_count, cycle_step, start_state)
    query_total, key_total, value_total = (final_state[2], final_state[3], final_state[4])
    d_query = (softmax_scale * query_total).astype(jnp.bfloat16).reshape(1, rows_here, proj_width)
    d_key = (softmax_scale * key_total).astype(jnp.bfloat16).reshape(1, rows_here, proj_width)
    d_value = value_total.astype(jnp.bfloat16).reshape(1, rows_here, proj_width)
    feature_cols = features[0]
    row_sums = lax.psum_scatter(
        jnp.einsum(
            "tf,tw->fw", feature_cols, d_value[0], preferred_element_type=jnp.float32
        ).astype(jnp.bfloat16),
        "fsdp",
        scatter_dimension=0,
        tiled=True,
    )
    weight_part = lax.psum_scatter(row_sums, "cp", scatter_dimension=1, tiled=True).astype(
        jnp.float32
    )
    return (d_query, d_key, d_value, weight_part)


def solution(mesh):
    return jax.shard_map(
        on_device,
        mesh=mesh,
        in_specs=(
            P("fsdp", "cp", None),
            P("fsdp", "cp", None),
            P("fsdp", "cp", None),
            P("fsdp", "cp", None),
            P("fsdp", "cp", None),
            P("fsdp", "cp", None),
            P("fsdp", "cp", None),
        ),
        out_specs=(
            P("fsdp", "cp", None),
            P("fsdp", "cp", None),
            P("fsdp", "cp", None),
            P("fsdp", "cp"),
        ),
        check_vma=False,
    )
```

profile of v0, /device:TPU:0, one launch (start us, length us, event | category | flops | bytes accessed | tf_op | source)
XLA Modules:
  0.0 243.9 jit_solution(6406590973211021745)
XLA Ops:
  7.3 0.7 copy.51
  8.0 14.8 %all_gather.6 = f32[1,512,10]{1,2,0:T(8,128)S(1)} all-gather(f32[1,128,10]{1,2,0:T(8,128)S(1)} %copy.51), channel_id=1, replica_groups=mesh['fsdp'=8,'cp'=4] {'cp'}, dimensions={1}, use_global_device_ids=true | all-gather | bytes 25600 | tf_op jit(solution)/shard_map/all_gather | solution.py:28
  22.8 1.2 copy.56
  24.0 1.9 copy.55
  25.9 1.2 copy.50
  27.1 0.2 copy.57
  27.3 1.2 copy.52
  28.5 0.9 copy.58
  29.4 1.2 copy.54
  30.7 13.1 %all-gather = f32[512,10]{0,1:T(8,128)S(1)} all-gather(f32[128,10]{0,1:T(8,128)S(1)} %reduce_sum.11), channel_id=2, replica_groups=mesh['fsdp'=8,'cp'=4] {'cp'}, dimensions={0}, use_global_device_ids=true | all-gather | bytes 25600 | tf_op jit(solution)/shard_map/all_gather | solution.py:29
  43.8 87.0 %while.24 = (s32[]{:T(128)}, bf16[1,128,1280]{1,2,0:T(8,128)(2,1)}, bf16[1,128,1280]{1,2,0:T(8,128)(2,1)S(1)}, f32[128,10,128]{2,0,1:T(8,128)}, f32[128,10,128]{...) while((s32[]{:T(128)}, bf16[1,128,1280]{1,2,0:T(8,128)(2,1)}, ...), condition=%wide.region_2.3_spmd.clone, body=%wide.region_1.2_spmd.clone.sunk | while | flops 212008976 | bytes 15104460 | solution.py:71
  43.8 1.0 copy.81
  44.8 1.6 collective-permute-start
  46.5 0.4 fusion.46
  46.9 1.4 fusion.47
  48.3 1.0 fusion.48
  49.2 2.9 %collective-permute-start.2 = (bf16[128,10,128]{2,0,1:T(8,128)(2,1)}, bf16[128,10,128]{2,0,1:T(8,128)(2,1)}, u32[]{:S(2)}, u32[]{:S(2)}) collective-permute-start(bf16[128,10,128]{2,0,1:T(8,128)(2,1)} %fusion.48), channel_id=1, source_target_pairs={{0,1},{1,2},{2,3},{3,0},{4,5},{5,6},{6,7},{7,4},{8,9},{9,10},{10,1... | collective-permute-start | bytes 983048 | tf_op jit(solution)/shard_map/while/body/eval_jaxpr/ppermute | solution.py:10
  52.1 1.2 fusion.49
  53.4 0.4 fusion.50
  53.8 11.1 %collective-permute-done.2 = bf16[128,10,128]{2,0,1:T(8,128)(2,1)} collective-permute-done((bf16[128,10,128]{2,0,1:T(8,128)(2,1)}, bf16[128,10,128]{2,0,1:T(8,128)(2,1)}, u32[]{:S(2)}, u32[]{:S(2)}) %collective-permute-start.2) | collective-permute-done | bytes 327712 | tf_op jit(solution)/shard_map/while/body/eval_jaxpr/ppermute | solution.py:10
  64.8 1.9 convert_element_type.94
  66.8 1.0 copy.81
  67.8 1.1 collective-permute-start.1
  69.0 0.4 fusion.46
  69.3 1.4 fusion.47
  70.7 2.1 fusion.48
  72.8 2.5 %collective-permute-start.2 = (bf16[128,10,128]{2,0,1:T(8,128)(2,1)}, bf16[128,10,128]{2,0,1:T(8,128)(2,1)}, u32[]{:S(2)}, u32[]{:S(2)}) collective-permute-start(bf16[128,10,128]{2,0,1:T(8,128)(2,1)} %fusion.48), channel_id=1, source_target_pairs={{0,1},{1,2},{2,3},{3,0},{4,5},{5,6},{6,7},{7,4},{8,9},{9,10},{10,1... | collective-permute-start | bytes 983048 | tf_op jit(solution)/shard_map/while/body/eval_jaxpr/ppermute | solution.py:10
  75.2 2.3 fusion.49
  77.6 0.4 fusion.50
  78.0 8.8 %collective-permute-done.2 = bf16[128,10,128]{2,0,1:T(8,128)(2,1)} collective-permute-done((bf16[128,10,128]{2,0,1:T(8,128)(2,1)}, bf16[128,10,128]{2,0,1:T(8,128)(2,1)}, u32[]{:S(2)}, u32[]{:S(2)}) %collective-permute-start.2) | collective-permute-done | bytes 327712 | tf_op jit(solution)/shard_map/while/body/eval_jaxpr/ppermute | solution.py:10
  86.8 1.9 convert_element_type.94
  88.7 1.0 copy.81
  89.7 1.2 collective-permute-start.1
  90.9 0.4 fusion.46
  91.3 1.4 fusion.47
  92.6 2.1 fusion.48
  94.7 2.5 %collective-permute-start.2 = (bf16[128,10,128]{2,0,1:T(8,128)(2,1)}, bf16[128,10,128]{2,0,1:T(8,128)(2,1)}, u32[]{:S(2)}, u32[]{:S(2)}) collective-permute-start(bf16[128,10,128]{2,0,1:T(8,128)(2,1)} %fusion.48), channel_id=1, source_target_pairs={{0,1},{1,2},{2,3},{3,0},{4,5},{5,6},{6,7},{7,4},{8,9},{9,10},{10,1... | collective-permute-start | bytes 983048 | tf_op jit(solution)/shard_map/while/body/eval_jaxpr/ppermute | solution.py:10
  97.2 2.3 fusion.49
  99.5 0.4 fusion.50
  99.9 8.8 %collective-permute-done.2 = bf16[128,10,128]{2,0,1:T(8,128)(2,1)} collective-permute-done((bf16[128,10,128]{2,0,1:T(8,128)(2,1)}, bf16[128,10,128]{2,0,1:T(8,128)(2,1)}, u32[]{:S(2)}, u32[]{:S(2)}) %collective-permute-start.2) | collective-permute-done | bytes 327712 | tf_op jit(solution)/shard_map/while/body/eval_jaxpr/ppermute | solution.py:10
  108.7 1.9 convert_element_type.94
  110.6 1.0 copy.81
  111.6 1.2 collective-permute-start.1
  112.8 0.4 fusion.46
  113.2 1.4 fusion.47
  114.5 2.1 fusion.48
  116.6 2.5 %collective-permute-start.2 = (bf16[128,10,128]{2,0,1:T(8,128)(2,1)}, bf16[128,10,128]{2,0,1:T(8,128)(2,1)}, u32[]{:S(2)}, u32[]{:S(2)}) collective-permute-start(bf16[128,10,128]{2,0,1:T(8,128)(2,1)} %fusion.48), channel_id=1, source_target_pairs={{0,1},{1,2},{2,3},{3,0},{4,5},{5,6},{6,7},{7,4},{8,9},{9,10},{10,1... | collective-permute-start | bytes 983048 | tf_op jit(solution)/shard_map/while/body/eval_jaxpr/ppermute | solution.py:10
  119.1 2.3 fusion.49
  121.4 0.4 fusion.50
  121.8 7.1 %collective-permute-done.2 = bf16[128,10,128]{2,0,1:T(8,128)(2,1)} collective-permute-done((bf16[128,10,128]{2,0,1:T(8,128)(2,1)}, bf16[128,10,128]{2,0,1:T(8,128)(2,1)}, u32[]{:S(2)}, u32[]{:S(2)}) %collective-permute-start.2) | collective-permute-done | bytes 327712 | tf_op jit(solution)/shard_map/while/body/eval_jaxpr/ppermute | solution.py:10
  128.9 1.9 convert_element_type.94
  130.8 0.2 copy.61
  131.0 4.6 %fusion.9 = bf16[2560,1280]{0,1:T(8,128)(2,1)} fusion(bf16[128,1280]{0,1:T(8,128)(2,1)S(1)} %bitcast.82, bf16[1,128,2560]{2,1,0:T(8,128)(2,1)S(1)} %copy-done), kind=kOutput, calls=%fused_computation.17 | convolution fusion | flops 842137600 | bytes 7536640 | tf_op jit(solution)/shard_map/tf,tw->fw/dot_general | solution.py:78
  135.6 9.5 %copy.72 = bf16[2560,1280]{1,0:T(8,128)(2,1)} copy(bf16[2560,1280]{0,1:T(8,128)(2,1)} %fusion.9) | data formatting | bytes 13107200
  145.2 61.4 %reduce-scatter.7.cloned.1.call-done = bf16[320,1280]{1,0:T(8,128)(2,1)} async-done(((bf16[2560,1280]{1,0:T(8,128)(2,1)}), bf16[320,1280]{1,0:T(8,128)(2,1)}) %reduce-scatter.7.cloned.1.call-update) | async-done | bytes 819216
  206.5 2.2 copy.73
  208.8 0.2 copy.59
  209.0 0.1 multiply_convert_fusion.1
  209.1 0.9 copy.62
  210.0 0.9 copy.64
  210.9 0.2 copy.60
  211.2 0.9 copy.63
  212.1 23.1 %reduce-scatter.5.cloned.1.call-done = bf16[320,320]{0,1:T(8,128)(2,1)} async-done(((bf16[320,1280]{0,1:T(8,128)(2,1)}), bf16[320,320]{0,1:T(8,128)(2,1)}) %reduce-scatter.5.cloned.1.call-update) | async-done | bytes 204816 | tf_op jit(solution)/shard_map/reduce_scatter | solution.py:85
  235.2 1.9 copy.65
  (36 shorter events, 0.6 us)
Async XLA Ops:
  7.2 123.9 %copy-start = (bf16[1,128,2560]{2,1,0:T(8,128)(2,1)S(1)}, bf16[1,128,2560]{2,1,0:T(8,128)(2,1)}, u32[]{:S(2)}) copy-start(bf16[1,128,2560]{2,1,0:T(8,128)(2,1)} %param.9) | copy-start | bytes 1966084
  7.2 199.4 %reduce-scatter.7.cloned.1.call-start = ((), (), s32[]{:S(2)}) async-start(), calls=%async_computation.3 | async-start | bytes 7372800
  44.8 21.9 %collective-permute-start = (bf16[1,128,1280]{1,2,0:T(8,128)(2,1)S(1)}, bf16[1,128,1280]{1,2,0:T(8,128)(2,1)}, u32[]{:S(2)}, u32[]{:S(2)}) collective-permute-start(bf16[1,128,1280]{1,2,0:T(8,128)(2,1)S(1)} %copy.81), channel_id=1, source_target_pairs={{0,1},{1,2},{2,3},{3,0},{4,5},{5,6},{6,7},{7,4},{8,9},{9,10},{10,1... | collective-permute-start | bytes 983048 | tf_op jit(solution)/shard_map/while/body/eval_jaxpr/ppermute | solution.py:10
  46.4 20.4 %collective-permute-start.1 = (bf16[1,128,1280]{1,2,0:T(8,128)(2,1)S(1)}, bf16[1,128,1280]{1,2,0:T(8,128)(2,1)S(1)}, u32[]{:S(2)}, u32[]{:S(2)}) collective-permute-start(bf16[1,128,1280]{1,2,0:T(8,128)(2,1)S(1)} %copy.82), channel_id=1, source_target_pairs={{0,1},{1,2},{2,3},{3,0},{4,5},{5,6},{6,7},{7,4},{8,9},{9,10},{10,1... | collective-permute-start | bytes 983048 | tf_op jit(solution)/shard_map/while/body/eval_jaxpr/ppermute | solution.py:10
  49.2 15.6 %collective-permute-start.2 = (bf16[128,10,128]{2,0,1:T(8,128)(2,1)}, bf16[128,10,128]{2,0,1:T(8,128)(2,1)}, u32[]{:S(2)}, u32[]{:S(2)}) collective-permute-start(bf16[128,10,128]{2,0,1:T(8,128)(2,1)} %fusion.48), channel_id=1, source_target_pairs={{0,1},{1,2},{2,3},{3,0},{4,5},{5,6},{6,7},{7,4},{8,9},{9,10},{10,1... | collective-permute-start | bytes 983048 | tf_op jit(solution)/shard_map/while/body/eval_jaxpr/ppermute | solution.py:10
  67.7 20.9 %collective-permute-start = (bf16[1,128,1280]{1,2,0:T(8,128)(2,1)S(1)}, bf16[1,128,1280]{1,2,0:T(8,128)(2,1)}, u32[]{:S(2)}, u32[]{:S(2)}) collective-permute-start(bf16[1,128,1280]{1,2,0:T(8,128)(2,1)S(1)} %copy.81), channel_id=1, source_target_pairs={{0,1},{1,2},{2,3},{3,0},{4,5},{5,6},{6,7},{7,4},{8,9},{9,10},{10,1... | collective-permute-start | bytes 983048 | tf_op jit(solution)/shard_map/while/body/eval_jaxpr/ppermute | solution.py:10
  67.8 20.9 %collective-permute-start.1 = (bf16[1,128,1280]{1,2,0:T(8,128)(2,1)S(1)}, bf16[1,128,1280]{1,2,0:T(8,128)(2,1)S(1)}, u32[]{:S(2)}, u32[]{:S(2)}) collective-permute-start(bf16[1,128,1280]{1,2,0:T(8,128)(2,1)S(1)} %copy.82), channel_id=1, source_target_pairs={{0,1},{1,2},{2,3},{3,0},{4,5},{5,6},{6,7},{7,4},{8,9},{9,10},{10,1... | collective-permute-start | bytes 983048 | tf_op jit(solution)/shard_map/while/body/eval_jaxpr/ppermute | solution.py:10
  72.8 14.0 %collective-permute-start.2 = (bf16[128,10,128]{2,0,1:T(8,128)(2,1)}, bf16[128,10,128]{2,0,1:T(8,128)(2,1)}, u32[]{:S(2)}, u32[]{:S(2)}) collective-permute-start(bf16[128,10,128]{2,0,1:T(8,128)(2,1)} %fusion.48), channel_id=1, source_target_pairs={{0,1},{1,2},{2,3},{3,0},{4,5},{5,6},{6,7},{7,4},{8,9},{9,10},{10,1... | collective-permute-start | bytes 983048 | tf_op jit(solution)/shard_map/while/body/eval_jaxpr/ppermute | solution.py:10
  89.7 20.9 %collective-permute-start = (bf16[1,128,1280]{1,2,0:T(8,128)(2,1)S(1)}, bf16[1,128,1280]{1,2,0:T(8,128)(2,1)}, u32[]{:S(2)}, u32[]{:S(2)}) collective-permute-start(bf16[1,128,1280]{1,2,0:T(8,128)(2,1)S(1)} %copy.81), channel_id=1, source_target_pairs={{0,1},{1,2},{2,3},{3,0},{4,5},{5,6},{6,7},{7,4},{8,9},{9,10},{10,1... | collective-permute-start | bytes 983048 | tf_op jit(solution)/shard_map/while/body/eval_jaxpr/ppermute | solution.py:10
  89.7 20.9 %collective-permute-start.1 = (bf16[1,128,1280]{1,2,0:T(8,128)(2,1)S(1)}, bf16[1,128,1280]{1,2,0:T(8,128)(2,1)S(1)}, u32[]{:S(2)}, u32[]{:S(2)}) collective-permute-start(bf16[1,128,1280]{1,2,0:T(8,128)(2,1)S(1)} %copy.82), channel_id=1, source_target_pairs={{0,1},{1,2},{2,3},{3,0},{4,5},{5,6},{6,7},{7,4},{8,9},{9,10},{10,1... | collective-permute-start | bytes 983048 | tf_op jit(solution)/shard_map/while/body/eval_jaxpr/ppermute | solution.py:10
  94.7 14.0 %collective-permute-start.2 = (bf16[128,10,128]{2,0,1:T(8,128)(2,1)}, bf16[128,10,128]{2,0,1:T(8,128)(2,1)}, u32[]{:S(2)}, u32[]{:S(2)}) collective-permute-start(bf16[128,10,128]{2,0,1:T(8,128)(2,1)} %fusion.48), channel_id=1, source_target_pairs={{0,1},{1,2},{2,3},{3,0},{4,5},{5,6},{6,7},{7,4},{8,9},{9,10},{10,1... | collective-permute-start | bytes 983048 | tf_op jit(solution)/shard_map/while/body/eval_jaxpr/ppermute | solution.py:10
  111.6 19.2 %collective-permute-start = (bf16[1,128,1280]{1,2,0:T(8,128)(2,1)S(1)}, bf16[1,128,1280]{1,2,0:T(8,128)(2,1)}, u32[]{:S(2)}, u32[]{:S(2)}) collective-permute-start(bf16[1,128,1280]{1,2,0:T(8,128)(2,1)S(1)} %copy.81), channel_id=1, source_target_pairs={{0,1},{1,2},{2,3},{3,0},{4,5},{5,6},{6,7},{7,4},{8,9},{9,10},{10,1... | collective-permute-start | bytes 983048 | tf_op jit(solution)/shard_map/while/body/eval_jaxpr/ppermute | solution.py:10
  111.6 19.2 %collective-permute-start.1 = (bf16[1,128,1280]{1,2,0:T(8,128)(2,1)S(1)}, bf16[1,128,1280]{1,2,0:T(8,128)(2,1)S(1)}, u32[]{:S(2)}, u32[]{:S(2)}) collective-permute-start(bf16[1,128,1280]{1,2,0:T(8,128)(2,1)S(1)} %copy.82), channel_id=1, source_target_pairs={{0,1},{1,2},{2,3},{3,0},{4,5},{5,6},{6,7},{7,4},{8,9},{9,10},{10,1... | collective-permute-start | bytes 983048 | tf_op jit(solution)/shard_map/while/body/eval_jaxpr/ppermute | solution.py:10
  116.6 12.3 %collective-permute-start.2 = (bf16[128,10,128]{2,0,1:T(8,128)(2,1)}, bf16[128,10,128]{2,0,1:T(8,128)(2,1)}, u32[]{:S(2)}, u32[]{:S(2)}) collective-permute-start(bf16[128,10,128]{2,0,1:T(8,128)(2,1)} %fusion.48), channel_id=1, source_target_pairs={{0,1},{1,2},{2,3},{3,0},{4,5},{5,6},{6,7},{7,4},{8,9},{9,10},{10,1... | collective-permute-start | bytes 983048 | tf_op jit(solution)/shard_map/while/body/eval_jaxpr/ppermute | solution.py:10
  145.1 63.7 %copy-start.2 = (f32[128,10,128]{2,0,1:T(8,128)S(1)}, f32[128,10,128]{2,0,1:T(8,128)}, u32[]{:S(2)}) copy-start(f32[128,10,128]{2,0,1:T(8,128)} %get-tuple-element.271) | copy-start | bytes 1966084
  145.1 65.8 %copy-start.1 = (f32[128,10,128]{2,0,1:T(8,128)S(1)}, f32[128,10,128]{2,0,1:T(8,128)}, u32[]{:S(2)}) copy-start(f32[128,10,128]{2,0,1:T(8,128)} %get-tuple-element.272) | copy-start | bytes 1966084
  145.1 90.1 %reduce-scatter.5.cloned.1.call-start = ((), (), s32[]{:S(2)}) async-start(), calls=%async_computation.2 | async-start | bytes 1228800 | tf_op jit(solution)/shard_map/reduce_scatter | solution.py:85
Sparse Core Ops, SparseCore 0:
  145.2 61.2 reduce-scatter.6
  208.9 26.2 reduce-scatter.4
where the time goes:
time: 245 us; the launch traced here: 244 us
  waiting for transfers between devices  120 us (49%)
  local copies, waits for them, and re-layouts  29.4 us (12%)
  matrix products  28.4 us (12%)
  blocking collectives  28 us (11%)
  starting transfers between devices  15.6 us (6%)
  between operations  14.2 us (6%)
  other arithmetic  7.92 us (3%)
    unnamed x3, waiting for transfers between devices  61.4 us
    ppermute x12, waiting for transfers between devices, passed_along(): return lax.ppermute(value, axis, pairs)  35.8 us
    unnamed x20, local copies, waits for them, and re-layouts  24.8 us
    reduce_scatter x1, waiting for transfers between devices, on_device(): lax.psum_scatter(row_sums, 'cp', scatter_dimension=1, tiled=True)  23.1 us
    ppermute x12, starting transfers between devices, passed_along(): return lax.ppermute(value, axis, pairs)  15.5 us
    all_gather x1, blocking collectives, on_device(): lax.all_gather(log_sums, 'cp', axis=1, tiled=True)  14.8 us
    all_gather x1, blocking collectives, on_device(): lax.all_gather(row_delta, 'cp', axis=1, tiled=True)  13.1 us
    dot_general x4, matrix products, cycle_step(): jnp.einsum('hqk,qhd->khd', grad_score, query_heads, preferred_element_typ...  8.16 us
  transfers between devices with their start and end apart: 14, of which 6 were waited for; matrix products, arithmetic and copies ran while one was open for 14% of the time, Pallas kernels for 0%

commit v1 on v0

--- a/solution.py
+++ b/solution.py
@@ -2,6 +2,18 @@
 import jax.numpy as jnp
 from jax import lax
 from jax.sharding import PartitionSpec as P
+
+
+def draft_bars(point, axis_key):
+    return jnp.concatenate(
+        jax.lax.all_to_all(
+            jnp.stack(tuple((point for _ in range(jax.lax.psum(1, axis_key)))), axis=0),
+            axis_key,
+            0,
+            0,
+        ),
+        axis=1,
+    )
 
 
 def passed_along(value, axis, steps):
@@ -25,7 +37,7 @@
     own_key = as_heads(key_rows)
     own_value = as_heads(value_rows)
     all_norms, all_deltas = (
-        lax.all_gather(log_sums, "cp", axis=1, tiled=True),
+        draft_bars(log_sums, "cp"),
         lax.all_gather(row_delta, "cp", axis=1, tiled=True),
     )
 

time: 245 us -> 244 us (level)
  blocking collectives: 28 us -> 13.7 us
  waiting for transfers between devices: 120 us -> 134 us
    all_gather x1 -> x0, blocking collectives: 14.8 us -> none  [on_device(): lax.all_gather(log_sums, 'cp', axis=1, tiled=True)]
    ppermute x12, waiting for transfers between devices: 35.8 us -> 49.2 us  [passed_along(): return lax.ppermute(value, axis, pairs)]
    ppermute x12, starting transfers between devices: 15.5 us -> 8.53 us  [passed_along(): return lax.ppermute(value, axis, pairs)]
    all_to_all x0 -> x1, starting transfers between devices: none -> 6.35 us  [draft_bars(): jax.lax.all_to_all(jnp.stack(tuple((point for _ in range(jax.lax.psum(1,...]
  transfers between devices with their start and end apart: 14 -> 15, of which waited for: 6 -> 6; matrix products, arithmetic and copies ran while one was open for 14% -> 18% of each run, Pallas kernels for 0% -> 0%
where the time goes in v1:
time: 244 us; the launch traced here: 243 us
  waiting for transfers between devices  134 us (55%)
  local copies, waits for them, and re-layouts  30.2 us (12%)
  matrix products  28.4 us (12%)
  starting transfers between devices  14.9 us (6%)
  between operations  14.2 us (6%)
  blocking collectives  13.7 us (6%)
  other arithmetic  7.89 us (3%)
    unnamed x3, waiting for transfers between devices  61.4 us
    ppermute x12, waiting for transfers between devices, passed_along(): return lax.ppermute(value, axis, pairs)  49.2 us
    unnamed x20, local copies, waits for them, and re-layouts  24.8 us
    reduce_scatter x1, waiting for transfers between devices, on_device(): lax.psum_scatter(row_sums, 'cp', scatter_dimension=1, tiled=True)  23 us
    all_gather x1, blocking collectives, on_device(): lax.all_gather(row_delta, 'cp', axis=1, tiled=True)  13.7 us
    ppermute x12, starting transfers between devices, passed_along(): return lax.ppermute(value, axis, pairs)  8.53 us
    dot_general x4, matrix products, cycle_step(): jnp.einsum('hqk,qhd->khd', grad_score, query_heads, preferred_element_typ...  8.13 us
    convert_element_type x4, other arithmetic, cycle_step(): passed_along(query_run.astype(jnp.bfloat16), 'cp', 1)  7.62 us
  transfers between devices with their start and end apart: 15, of which 6 were waited for; matrix products, arithmetic and copies ran while one was open for 18% of the time, Pallas kernels for 0%

profile of v1, /device:TPU:0, one launch (start us, length us, event | category | flops | bytes accessed | tf_op | source)
XLA Modules:
  0.0 243.1 jit_solution(9632144444445845076)
XLA Ops:
  7.2 0.8 copy.79
  7.9 0.6 stack.2
  8.6 6.3 %all-to-all-start = ((f32[4,1,128,10]{2,1,3,0:T(1,128)}), f32[4,1,128,10]{2,1,3,0:T(1,128)S(1)}, u32[]{:S(2)}, u32[]{:S(2)}) async-start(f32[4,1,128,10]{2,1,3,0:T(1,128)} %stack.2), calls=%async_computation | async-start | bytes 40960 | tf_op jit(solution)/shard_map/all_to_all | solution.py:9
  14.9 1.2 copy.55
  16.1 1.2 copy.53
  17.4 1.9 copy.54
  19.3 1.2 copy.49
  20.4 0.2 copy.56
  20.7 1.2 copy.51
  21.9 0.9 copy.58
  22.8 13.7 %all-gather = f32[512,10]{0,1:T(8,128)S(1)} all-gather(f32[128,10]{0,1:T(8,128)S(1)} %reduce_sum.11), channel_id=2, replica_groups=mesh['fsdp'=8,'cp'=4] {'cp'}, dimensions={0}, use_global_device_ids=true | all-gather | bytes 25600 | tf_op jit(solution)/shard_map/all_gather | solution.py:41
  36.5 93.6 %while.24 = (s32[]{:T(128)}, bf16[1,128,1280]{1,2,0:T(8,128)(2,1)}, bf16[1,128,1280]{1,2,0:T(8,128)(2,1)S(1)}, f32[128,10,128]{2,0,1:T(8,128)}, f32[128,10,128]{...) while((s32[]{:T(128)}, bf16[1,128,1280]{1,2,0:T(8,128)(2,1)}, ...), condition=%wide.region_2.3_spmd.clone, body=%wide.region_1.2_spmd.clone.sunk | while | flops 212008976 | bytes 15114704 | solution.py:83
  36.5 1.0 copy.89
  37.5 1.5 collective-permute-start
  39.2 0.4 fusion.46
  39.5 1.4 fusion.47
  40.9 1.0 fusion.48
  41.9 2.9 %collective-permute-start.2 = (bf16[128,10,128]{2,0,1:T(8,128)(2,1)}, bf16[128,10,128]{2,0,1:T(8,128)(2,1)}, u32[]{:S(2)}, u32[]{:S(2)}) collective-permute-start(bf16[128,10,128]{2,0,1:T(8,128)(2,1)} %fusion.48), channel_id=1, source_target_pairs={{0,1},{1,2},{2,3},{3,0},{4,5},{5,6},{6,7},{7,4},{8,9},{9,10},{10,1... | collective-permute-start | bytes 983048 | tf_op jit(solution)/shard_map/while/body/eval_jaxpr/ppermute | solution.py:22
  44.7 1.2 fusion.49
  46.0 0.4 fusion.50
  46.4 13.1 %collective-permute-done.2 = bf16[128,10,128]{2,0,1:T(8,128)(2,1)} collective-permute-done((bf16[128,10,128]{2,0,1:T(8,128)(2,1)}, bf16[128,10,128]{2,0,1:T(8,128)(2,1)}, u32[]{:S(2)}, u32[]{:S(2)}) %collective-permute-start.2) | collective-permute-done | bytes 327712 | tf_op jit(solution)/shard_map/while/body/eval_jaxpr/ppermute | solution.py:22
  59.5 1.9 convert_element_type.94
  61.4 1.0 copy.89
  62.4 0.2 collective-permute-start.1
  62.6 0.4 fusion.46
  63.0 1.4 fusion.47
  64.3 2.1 fusion.48
  66.4 2.5 %collective-permute-start.2 = (bf16[128,10,128]{2,0,1:T(8,128)(2,1)}, bf16[128,10,128]{2,0,1:T(8,128)(2,1)}, u32[]{:S(2)}, u32[]{:S(2)}) collective-permute-start(bf16[128,10,128]{2,0,1:T(8,128)(2,1)} %fusion.48), channel_id=1, source_target_pairs={{0,1},{1,2},{2,3},{3,0},{4,5},{5,6},{6,7},{7,4},{8,9},{9,10},{10,1... | collective-permute-start | bytes 983048 | tf_op jit(solution)/shard_map/while/body/eval_jaxpr/ppermute | solution.py:22
  68.9 2.3 fusion.49
  71.2 0.4 fusion.50
  71.6 11.8 %collective-permute-done.2 = bf16[128,10,128]{2,0,1:T(8,128)(2,1)} collective-permute-done((bf16[128,10,128]{2,0,1:T(8,128)(2,1)}, bf16[128,10,128]{2,0,1:T(8,128)(2,1)}, u32[]{:S(2)}, u32[]{:S(2)}) %collective-permute-start.2) | collective-permute-done | bytes 327712 | tf_op jit(solution)/shard_map/while/body/eval_jaxpr/ppermute | solution.py:22
  83.3 1.9 convert_element_type.94
  85.2 1.0 copy.89
  86.4 0.4 fusion.46
  86.8 1.4 fusion.47
  88.1 2.1 fusion.48
  90.2 0.7 collective-permute-start.2
  90.9 2.3 fusion.49
  93.2 0.4 fusion.50
  93.6 12.6 %collective-permute-done.2 = bf16[128,10,128]{2,0,1:T(8,128)(2,1)} collective-permute-done((bf16[128,10,128]{2,0,1:T(8,128)(2,1)}, bf16[128,10,128]{2,0,1:T(8,128)(2,1)}, u32[]{:S(2)}, u32[]{:S(2)}) %collective-permute-start.2) | collective-permute-done | bytes 327712 | tf_op jit(solution)/shard_map/while/body/eval_jaxpr/ppermute | solution.py:22
  106.2 1.9 convert_element_type.94
  108.2 1.0 copy.89
  109.3 0.4 fusion.46
  109.7 1.4 fusion.47
  111.0 2.1 fusion.48
  113.1 0.6 collective-permute-start.2
  113.7 2.3 fusion.49
  116.0 0.4 fusion.50
  116.4 11.8 %collective-permute-done.2 = bf16[128,10,128]{2,0,1:T(8,128)(2,1)} collective-permute-done((bf16[128,10,128]{2,0,1:T(8,128)(2,1)}, bf16[128,10,128]{2,0,1:T(8,128)(2,1)}, u32[]{:S(2)}, u32[]{:S(2)}) %collective-permute-start.2) | collective-permute-done | bytes 327712 | tf_op jit(solution)/shard_map/while/body/eval_jaxpr/ppermute | solution.py:22
  128.2 1.9 convert_element_type.94
  130.1 0.2 copy.61
  130.3 4.6 %fusion.9 = bf16[2560,1280]{0,1:T(8,128)(2,1)} fusion(bf16[128,1280]{0,1:T(8,128)(2,1)S(1)} %bitcast.89, bf16[1,128,2560]{2,1,0:T(8,128)(2,1)S(1)} %copy-done), kind=kOutput, calls=%fused_computation.18 | convolution fusion | flops 842137600 | bytes 7536640 | tf_op jit(solution)/shard_map/tf,tw->fw/dot_general | solution.py:90
  134.9 9.5 %copy.72 = bf16[2560,1280]{1,0:T(8,128)(2,1)} copy(bf16[2560,1280]{0,1:T(8,128)(2,1)} %fusion.9) | data formatting | bytes 13107200
  144.5 61.3 %reduce-scatter.7.cloned.1.call-done = bf16[320,1280]{1,0:T(8,128)(2,1)} async-done(((bf16[2560,1280]{1,0:T(8,128)(2,1)}), bf16[320,1280]{1,0:T(8,128)(2,1)}) %reduce-scatter.7.cloned.1.call-update) | async-done | bytes 819216
  205.8 2.2 copy.73
  208.0 0.2 copy.59
  208.3 0.1 multiply_convert_fusion.1
  208.4 0.9 copy.62
  209.3 0.9 copy.64
  210.2 0.2 copy.60
  210.4 0.1 multiply_convert_fusion
  210.5 0.9 copy.63
  211.4 23.0 %reduce-scatter.5.cloned.1.call-done = bf16[320,320]{0,1:T(8,128)(2,1)} async-done(((bf16[320,1280]{0,1:T(8,128)(2,1)}), bf16[320,320]{0,1:T(8,128)(2,1)}) %reduce-scatter.5.cloned.1.call-update) | async-done | bytes 204816 | tf_op jit(solution)/shard_map/reduce_scatter | solution.py:97
  234.4 1.9 copy.65
  (47 shorter events, 0.6 us)
Async XLA Ops:
  7.2 123.2 %copy-start = (bf16[1,128,2560]{2,1,0:T(8,128)(2,1)S(1)}, bf16[1,128,2560]{2,1,0:T(8,128)(2,1)}, u32[]{:S(2)}) copy-start(bf16[1,128,2560]{2,1,0:T(8,128)(2,1)} %param.9) | copy-start | bytes 1966084
  8.6 27.9 %all-to-all-start = ((f32[4,1,128,10]{2,1,3,0:T(1,128)}), f32[4,1,128,10]{2,1,3,0:T(1,128)S(1)}, u32[]{:S(2)}, u32[]{:S(2)}) async-start(f32[4,1,128,10]{2,1,3,0:T(1,128)} %stack.2), calls=%async_computation | async-start | bytes 40960 | tf_op jit(solution)/shard_map/all_to_all | solution.py:9
  14.9 190.9 %reduce-scatter.7.cloned.1.call-start = ((), (), s32[]{:S(2)}) async-start(), calls=%async_computation.4 | async-start | bytes 7372800
  37.5 23.9 %collective-permute-start = (bf16[1,128,1280]{1,2,0:T(8,128)(2,1)S(1)}, bf16[1,128,1280]{1,2,0:T(8,128)(2,1)}, u32[]{:S(2)}, u32[]{:S(2)}) collective-permute-start(bf16[1,128,1280]{1,2,0:T(8,128)(2,1)S(1)} %copy.89), channel_id=1, source_target_pairs={{0,1},{1,2},{2,3},{3,0},{4,5},{5,6},{6,7},{7,4},{8,9},{9,10},{10,1... | collective-permute-start | bytes 983048 | tf_op jit(solution)/shard_map/while/body/eval_jaxpr/ppermute | solution.py:22
  39.0 22.4 %collective-permute-start.1 = (bf16[1,128,1280]{1,2,0:T(8,128)(2,1)S(1)}, bf16[1,128,1280]{1,2,0:T(8,128)(2,1)S(1)}, u32[]{:S(2)}, u32[]{:S(2)}) collective-permute-start(bf16[1,128,1280]{1,2,0:T(8,128)(2,1)S(1)} %copy.90), channel_id=1, source_target_pairs={{0,1},{1,2},{2,3},{3,0},{4,5},{5,6},{6,7},{7,4},{8,9},{9,10},{10,1... | collective-permute-start | bytes 983048 | tf_op jit(solution)/shard_map/while/body/eval_jaxpr/ppermute | solution.py:22
  41.9 17.6 %collective-permute-start.2 = (bf16[128,10,128]{2,0,1:T(8,128)(2,1)}, bf16[128,10,128]{2,0,1:T(8,128)(2,1)}, u32[]{:S(2)}, u32[]{:S(2)}) collective-permute-start(bf16[128,10,128]{2,0,1:T(8,128)(2,1)} %fusion.48), channel_id=1, source_target_pairs={{0,1},{1,2},{2,3},{3,0},{4,5},{5,6},{6,7},{7,4},{8,9},{9,10},{10,1... | collective-permute-start | bytes 983048 | tf_op jit(solution)/shard_map/while/body/eval_jaxpr/ppermute | solution.py:22
  62.3 22.9 %collective-permute-start = (bf16[1,128,1280]{1,2,0:T(8,128)(2,1)S(1)}, bf16[1,128,1280]{1,2,0:T(8,128)(2,1)}, u32[]{:S(2)}, u32[]{:S(2)}) collective-permute-start(bf16[1,128,1280]{1,2,0:T(8,128)(2,1)S(1)} %copy.89), channel_id=1, source_target_pairs={{0,1},{1,2},{2,3},{3,0},{4,5},{5,6},{6,7},{7,4},{8,9},{9,10},{10,1... | collective-permute-start | bytes 983048 | tf_op jit(solution)/shard_map/while/body/eval_jaxpr/ppermute | solution.py:22
  62.4 22.9 %collective-permute-start.1 = (bf16[1,128,1280]{1,2,0:T(8,128)(2,1)S(1)}, bf16[1,128,1280]{1,2,0:T(8,128)(2,1)S(1)}, u32[]{:S(2)}, u32[]{:S(2)}) collective-permute-start(bf16[1,128,1280]{1,2,0:T(8,128)(2,1)S(1)} %copy.90), channel_id=1, source_target_pairs={{0,1},{1,2},{2,3},{3,0},{4,5},{5,6},{6,7},{7,4},{8,9},{9,10},{10,1... | collective-permute-start | bytes 983048 | tf_op jit(solution)/shard_map/while/body/eval_jaxpr/ppermute | solution.py:22
  66.4 17.0 %collective-permute-start.2 = (bf16[128,10,128]{2,0,1:T(8,128)(2,1)}, bf16[128,10,128]{2,0,1:T(8,128)(2,1)}, u32[]{:S(2)}, u32[]{:S(2)}) collective-permute-start(bf16[128,10,128]{2,0,1:T(8,128)(2,1)} %fusion.48), channel_id=1, source_target_pairs={{0,1},{1,2},{2,3},{3,0},{4,5},{5,6},{6,7},{7,4},{8,9},{9,10},{10,1... | collective-permute-start | bytes 983048 | tf_op jit(solution)/shard_map/while/body/eval_jaxpr/ppermute | solution.py:22
  86.2 21.9 %collective-permute-start = (bf16[1,128,1280]{1,2,0:T(8,128)(2,1)S(1)}, bf16[1,128,1280]{1,2,0:T(8,128)(2,1)}, u32[]{:S(2)}, u32[]{:S(2)}) collective-permute-start(bf16[1,128,1280]{1,2,0:T(8,128)(2,1)S(1)} %copy.89), channel_id=1, source_target_pairs={{0,1},{1,2},{2,3},{3,0},{4,5},{5,6},{6,7},{7,4},{8,9},{9,10},{10,1... | collective-permute-start | bytes 983048 | tf_op jit(solution)/shard_map/while/body/eval_jaxpr/ppermute | solution.py:22
  86.2 21.9 %collective-permute-start.1 = (bf16[1,128,1280]{1,2,0:T(8,128)(2,1)S(1)}, bf16[1,128,1280]{1,2,0:T(8,128)(2,1)S(1)}, u32[]{:S(2)}, u32[]{:S(2)}) collective-permute-start(bf16[1,128,1280]{1,2,0:T(8,128)(2,1)S(1)} %copy.90), channel_id=1, source_target_pairs={{0,1},{1,2},{2,3},{3,0},{4,5},{5,6},{6,7},{7,4},{8,9},{9,10},{10,1... | collective-permute-start | bytes 983048 | tf_op jit(solution)/shard_map/while/body/eval_jaxpr/ppermute | solution.py:22
  90.2 16.0 %collective-permute-start.2 = (bf16[128,10,128]{2,0,1:T(8,128)(2,1)}, bf16[128,10,128]{2,0,1:T(8,128)(2,1)}, u32[]{:S(2)}, u32[]{:S(2)}) collective-permute-start(bf16[128,10,128]{2,0,1:T(8,128)(2,1)} %fusion.48), channel_id=1, source_target_pairs={{0,1},{1,2},{2,3},{3,0},{4,5},{5,6},{6,7},{7,4},{8,9},{9,10},{10,1... | collective-permute-start | bytes 983048 | tf_op jit(solution)/shard_map/while/body/eval_jaxpr/ppermute | solution.py:22
  109.1 21.0 %collective-permute-start = (bf16[1,128,1280]{1,2,0:T(8,128)(2,1)S(1)}, bf16[1,128,1280]{1,2,0:T(8,128)(2,1)}, u32[]{:S(2)}, u32[]{:S(2)}) collective-permute-start(bf16[1,128,1280]{1,2,0:T(8,128)(2,1)S(1)} %copy.89), channel_id=1, source_target_pairs={{0,1},{1,2},{2,3},{3,0},{4,5},{5,6},{6,7},{7,4},{8,9},{9,10},{10,1... | collective-permute-start | bytes 983048 | tf_op jit(solution)/shard_map/while/body/eval_jaxpr/ppermute | solution.py:22
  109.2 20.9 %collective-permute-start.1 = (bf16[1,128,1280]{1,2,0:T(8,128)(2,1)S(1)}, bf16[1,128,1280]{1,2,0:T(8,128)(2,1)S(1)}, u32[]{:S(2)}, u32[]{:S(2)}) collective-permute-start(bf16[1,128,1280]{1,2,0:T(8,128)(2,1)S(1)} %copy.90), channel_id=1, source_target_pairs={{0,1},{1,2},{2,3},{3,0},{4,5},{5,6},{6,7},{7,4},{8,9},{9,10},{10,1... | collective-permute-start | bytes 983048 | tf_op jit(solution)/shard_map/while/body/eval_jaxpr/ppermute | solution.py:22
  113.1 15.1 %collective-permute-start.2 = (bf16[128,10,128]{2,0,1:T(8,128)(2,1)}, bf16[128,10,128]{2,0,1:T(8,128)(2,1)}, u32[]{:S(2)}, u32[]{:S(2)}) collective-permute-start(bf16[128,10,128]{2,0,1:T(8,128)(2,1)} %fusion.48), channel_id=1, source_target_pairs={{0,1},{1,2},{2,3},{3,0},{4,5},{5,6},{6,7},{7,4},{8,9},{9,10},{10,1... | collective-permute-start | bytes 983048 | tf_op jit(solution)/shard_map/while/body/eval_jaxpr/ppermute | solution.py:22
  144.4 63.6 %copy-start.2 = (f32[128,10,128]{2,0,1:T(8,128)S(1)}, f32[128,10,128]{2,0,1:T(8,128)}, u32[]{:S(2)}) copy-start(f32[128,10,128]{2,0,1:T(8,128)} %get-tuple-element.271) | copy-start | bytes 1966084
  144.4 65.8 %copy-start.1 = (f32[128,10,128]{2,0,1:T(8,128)S(1)}, f32[128,10,128]{2,0,1:T(8,128)}, u32[]{:S(2)}) copy-start(f32[128,10,128]{2,0,1:T(8,128)} %get-tuple-element.272) | copy-start | bytes 1966084
  144.4 90.0 %reduce-scatter.5.cloned.1.call-start = ((), (), s32[]{:S(2)}) async-start(), calls=%async_computation.3 | async-start | bytes 1228800 | tf_op jit(solution)/shard_map/reduce_scatter | solution.py:97
Sparse Core Ops, SparseCore 0:
  144.5 61.2 reduce-scatter.6
  208.1 26.2 reduce-scatter.4
